TPU v7x, 256 devices: a whole 4x4x8 slice. The times are simulated.
256 devices in a mesh: ctx: 32 (over x_hi, z, core), head: 8 (over x_lo, y).
Axes of the slice: x: 4 (x_hi: 2, x_lo: 2; x = x_hi * 2 + x_lo), y: 4, z: 8, core: 2. Of those that a mesh axis runs over, the one named last changes fastest.
Arguments:
- queries: bfloat16 [6656, 4096], P('ctx', 'head'), may hold values from -4 to 4
- rotated_key_rows: bfloat16 [6656, 1024], P('ctx', 'head'), may hold values from -4 to 4
- value_matrix: bfloat16 [6656, 1024], P('ctx', 'head'), may hold values from -4 to 4
- out_grad: bfloat16 [6656, 4096], P('ctx', 'head'), may hold values from -6 to 6
- w_out: bfloat16 [4096, 4096], P('head'), may hold values from -0.09375 to 0.09375
- doc_lengths: int32 [16], replicated, may hold values from 1 to 3744, 6656 in all
Outputs:
- grad_q: bfloat16 [6656, 4096], P('ctx', 'head')
- key_gradient: bfloat16 [6656, 1024], P('ctx', 'head')
- value_gradient: bfloat16 [6656, 1024], P('ctx', 'head')
- grad_wo_t: bfloat16 [4096, 4096], P('ctx', 'head')
Inputs may be any that keep to these rules, and one draw needn't show every extreme that they name: `doc_lengths`: 16 lengths summing to 6656; the longest is exactly 3744.
All inputs are finite; a program needn't handle non-finite values.
Results may differ from a plain program's by a relative error of at most 0.019.
Values may be sent and summed in bfloat16 or wider, within the bound.
A program may use at most 128 MiB of HBM per device.

v0:
```python
import jax
import jax.numpy as jnp
from jax import lax
from jax.sharding import PartitionSpec as P

HEAD_SIZE = 128


def per_device(queries, rotated_key_rows, value_matrix, out_grad, w_out, doc_lengths):
    tok_rows = queries.shape[0]
    q_heads = queries.shape[1] // HEAD_SIZE
    kv_heads = rotated_key_rows.shape[1] // HEAD_SIZE
    query_group_width = q_heads // kv_heads
    key_width = kv_heads * HEAD_SIZE
    logit_scale = HEAD_SIZE ** (-0.5)
    ctx_count = lax.axis_size("ctx")
    total_rows = tok_rows * ctx_count
    my_first = lax.axis_index("ctx") * tok_rows
    hi_pos = my_first + tok_rows - 1
    doc_ends = jnp.cumsum(doc_lengths)
    my_positions = my_first + jnp.arange(tok_rows, dtype=jnp.int32)
    my_segs = jnp.sum(
        jnp.where(doc_ends[None, :] <= my_positions[:, None], doc_lengths[None, :], 0), axis=1
    )
    lo_seg = jnp.min(my_segs)
    q_tiles = queries.reshape(tok_rows, kv_heads, query_group_width, HEAD_SIZE)
    key_all, value_all = (
        lax.all_gather(rotated_key_rows, "ctx", axis=0, tiled=True),
        lax.all_gather(value_matrix, "ctx", axis=0, tiled=True),
    )
    grad_cols = lax.all_gather(out_grad, "head", axis=1, tiled=True)
    key_block = 512
    block_count = total_rows // key_block

    def masked(q_pos, q_seg, key_pos):
        allowed = (key_pos[None, :] <= q_pos[:, None]) & (key_pos[None, :] >= q_seg[:, None])
        return allowed[None, :, None, :]

    def key_slice(block_index):
        offset = block_index * key_block
        key_tile = lax.dynamic_slice_in_dim(key_all, offset, key_block, 0).reshape(
            key_block, kv_heads, HEAD_SIZE
        )
        value_tile = lax.dynamic_slice_in_dim(value_all, offset, key_block, 0).reshape(
            key_block, kv_heads, HEAD_SIZE
        )
        key_pos = offset + jnp.arange(key_block, dtype=jnp.int32)
        active = (offset <= hi_pos) & (offset + key_block - 1 >= lo_seg)
        return (offset, key_tile, value_tile, key_pos, active)

    def forward_step(block_index, loop_state):
        offset, key_tile, value_tile, key_pos, active = key_slice(block_index)
        weighted, totals = loop_state
        scores = (
            jnp.einsum("tgrd,kgd->gtrk", q_tiles, key_tile, preferred_element_type=jnp.float32)
            * logit_scale
        )
        expo_vals = jnp.where(masked(my_positions, my_segs, key_pos), jnp.exp(scores), 0.0)
        weighted = weighted + jnp.einsum(
            "gtrk,kgd->tgrd",
            expo_vals.astype(jnp.bfloat16),
            value_tile,
            preferred_element_type=jnp.float32,
        )
        return (weighted, totals + jnp.sum(expo_vals, axis=3))

    start_state = (
        jnp.zeros((tok_rows, kv_heads, query_group_width, HEAD_SIZE), jnp.float32),
        jnp.zeros((kv_heads, tok_rows, query_group_width), jnp.float32),
    )
    weighted, totals = lax.fori_loop(0, block_count, forward_step, start_state)
    attn_tiles = (weighted / jnp.transpose(totals, (1, 0, 2))[..., None]).astype(jnp.bfloat16)
    log_total = jnp.log(totals)
    attn_flat = attn_tiles.reshape(tok_rows, q_heads * HEAD_SIZE)
    grad_attn = lax.dot_general(
        grad_cols, w_out, (((1,), (1,)), ((), ())), preferred_element_type=jnp.float32
    ).astype(jnp.bfloat16)
    grad_tiles = grad_attn.reshape(tok_rows, kv_heads, query_group_width, HEAD_SIZE)
    row_delta = jnp.transpose(
        jnp.sum(grad_tiles.astype(jnp.float32) * attn_tiles.astype(jnp.float32), axis=3), (1, 0, 2)
    )

    def grad_tile(q_part, g_part, lt_part, rd_part, q_pos, q_seg, key_tile, value_tile, key_pos):
        allowed = masked(q_pos, q_seg, key_pos)
        scores = (
            jnp.einsum("tgrd,kgd->gtrk", q_part, key_tile, preferred_element_type=jnp.float32)
            * logit_scale
        )
        attn_weights = jnp.where(allowed, jnp.exp(scores - lt_part[..., None]), 0.0)
        grad_weights = jnp.einsum(
            "tgrd,kgd->gtrk", g_part, value_tile, preferred_element_type=jnp.float32
        )
        dscore = (attn_weights * (grad_weights - rd_part[..., None])).astype(jnp.bfloat16)
        dq_term = jnp.einsum("gtrk,kgd->tgrd", dscore, key_tile, preferred_element_type=jnp.float32)
        dk_term = jnp.einsum("gtrk,tgrd->kgd", dscore, q_part, preferred_element_type=jnp.float32)
        dv_term = jnp.einsum(
            "gtrk,tgrd->kgd",
            attn_weights.astype(jnp.bfloat16),
            g_part,
            preferred_element_type=jnp.float32,
        )
        return (dq_term, dk_term, dv_term)

    zero_q = jnp.zeros((tok_rows, kv_heads, query_group_width, HEAD_SIZE), jnp.float32)

    def backward_step(block_index, loop_state):
        offset, key_tile, value_tile, key_pos, active = key_slice(block_index)
        q_accum, kv_accum = loop_state
        dq_term, dk_term, dv_term = grad_tile(
            q_tiles,
            grad_tiles,
            log_total,
            row_delta,
            my_positions,
            my_segs,
            key_tile,
            value_tile,
            key_pos,
        )
        joined = jnp.concatenate(
            [dk_term.reshape(key_block, key_width), dv_term.reshape(key_block, key_width)], axis=1
        )
        return (q_accum + dq_term, lax.dynamic_update_slice_in_dim(kv_accum, joined, offset, 0))

    q_accum, kv_accum = lax.fori_loop(
        0, block_count, backward_step, (zero_q, jnp.zeros((total_rows, 2 * key_width), jnp.float32))
    )
    own_grads = lax.psum_scatter(
        kv_accum.astype(jnp.bfloat16), "ctx", scatter_dimension=0, tiled=True
    ).astype(jnp.float32)
    key_gradient = (logit_scale * own_grads[:, :key_width]).astype(jnp.bfloat16)
    value_gradient = own_grads[:, key_width:].astype(jnp.bfloat16)
    grad_wo = lax.psum_scatter(
        lax.dot_general(
            grad_cols, attn_flat, (((0,), (0,)), ((), ())), preferred_element_type=jnp.float32
        ).astype(jnp.bfloat16),
        "ctx",
        scatter_dimension=0,
        tiled=True,
    )
    grad_q = (logit_scale * q_accum).reshape(tok_rows, q_heads * HEAD_SIZE).astype(jnp.bfloat16)
    return (grad_q, key_gradient, value_gradient, grad_wo)


def solution(mesh):
    return jax.shard_map(
        per_device,
        mesh=mesh,
        in_specs=(
            P("ctx", "head"),
            P("ctx", "head"),
            P("ctx", "head"),
            P("ctx", "head"),
            P("head", None),
            P(),
        ),
        out_specs=(P("ctx", "head"), P("ctx", "head"), P("ctx", "head"), P("ctx", "head")),
        check_vma=False,
    )
```

profile of v0, /device:TPU:8, one launch (start us, length us, event | category | flops | bytes accessed | tf_op | source)
XLA Modules:
  0.0 594.3 jit_solution(7932197649029800151)
XLA Ops:
  12.1 41.0 %all-gather.8.cloned.1.call-done = bf16[208,4096]{1,0:T(8,128)(2,1)} async-done(((bf16[208,512]{1,0:T(8,128)(2,1)}), bf16[208,4096]{1,0:T(8,128)(2,1)}) %all-gather.8.cloned.1.call-update) | async-done | bytes 1703952 | tf_op jit(solution)/shard_map/all_gather | solution.py:31
  53.2 4.2 convolution_convert_fusion.1
  57.5 79.3 %all-gather.4.cloned.1.call-done = bf16[6656,128]{1,0:T(8,128)(2,1)} async-done(((bf16[208,128]{1,0:T(8,128)(2,1)}), bf16[6656,128]{1,0:T(8,128)(2,1)}) %all-gather.4.cloned.1.call-update) | async-done | bytes 1703952 | tf_op jit(solution)/shard_map/all_gather | solution.py:28
  136.8 78.0 %all-gather.6.cloned.1.call-done = bf16[6656,128]{1,0:T(8,128)(2,1)} async-done(((bf16[208,128]{1,0:T(8,128)(2,1)}), bf16[6656,128]{1,0:T(8,128)(2,1)}) %all-gather.6.cloned.1.call-update) | async-done | bytes 1703952 | tf_op jit(solution)/shard_map/all_gather | solution.py:29
  214.9 41.1 %while.32 = (s32[]{:T(128)}, f32[208,1,4,128]{3,0,2,1:T(8,128)S(1)}, f32[1,208,4]{1,2,0:T(4,128)S(1)}, bf16[6656,128]{1,0:T(8,128)(2,1)}, s32[208]{0:T(256)S(1)}...) while((s32[]{:T(128)}, ...), condition=%wide.region_4.5_spmd.clone, body=%wide.region_2.4_spmd.clone.sunk | while | flops 220341792 | bytes 3264134 | solution.py:71
  215.0 1.6 fusion.57
  216.6 1.4 fusion.58
  218.2 1.6 fusion.57
  221.4 1.6 fusion.57
  224.5 1.6 fusion.57
  226.1 1.4 fusion.58
  227.7 1.6 fusion.57
  230.8 1.6 fusion.57
  234.0 1.6 fusion.57
  237.2 1.6 fusion.57
  238.7 1.4 fusion.58
  240.3 1.6 fusion.57
  243.5 1.6 fusion.57
  246.7 1.6 fusion.57
  249.8 1.6 fusion.57
  251.4 1.4 fusion.58
  253.0 1.6 fusion.57
  256.3 2.0 broadcast_in_dim.86.clone
  258.4 76.8 %while.33 = (s32[]{:T(128)}, f32[208,1,4,128]{3,0,2,1:T(8,128)S(1)}, bf16[6656,256]{1,0:T(8,128)(2,1)}, bf16[6656,128]{1,0:T(8,128)(2,1)}, s32[208]{0:T(256)S(1)...) while((s32[]{:T(128)}, ...), condition=%wide.region_7.8_spmd.clone, body=%wide.region_6.7_spmd.clone.sunk | while | flops 549298944 | bytes 11826341 | solution.py:125
  258.5 1.5 bitcast_select_fusion.3
  264.5 1.5 bitcast_select_fusion.3
  267.9 1.4 fusion.70
  270.4 1.5 bitcast_select_fusion.3
  276.3 1.5 bitcast_select_fusion.3
  282.2 1.5 bitcast_select_fusion.3
  288.1 1.5 bitcast_select_fusion.3
  294.0 1.5 bitcast_select_fusion.3
  297.5 1.4 fusion.70
  299.9 1.5 bitcast_select_fusion.3
  303.4 1.4 fusion.70
  305.9 1.5 bitcast_select_fusion.3
  311.8 1.5 bitcast_select_fusion.3
  317.7 1.5 bitcast_select_fusion.3
  321.2 1.4 fusion.70
  323.6 1.5 bitcast_select_fusion.3
  329.5 1.5 bitcast_select_fusion.3
  333.0 1.4 fusion.70
  336.7 3.3 fusion.29
  339.9 6.5 %copy.43 = bf16[4096,512]{1,0:T(8,128)(2,1)} copy(bf16[4096,512]{0,1:T(8,128)(2,1)} %fusion.29) | data formatting | bytes 8388608
  347.3 109.5 %reduce-scatter.5.cloned.1.call-done = bf16[208,256]{1,0:T(8,128)(2,1)} async-done(((bf16[6656,256]{1,0:T(8,128)(2,1)}), bf16[208,256]{1,0:T(8,128)(2,1)}) %reduce-scatter.5.cloned.1.call-update) | async-done | bytes 106512 | tf_op jit(solution)/shard_map/reduce_scatter | solution.py:128
  456.8 1.4 slice.14
  458.3 1.4 multiply_convert_fusion.1
  459.7 128.1 %reduce-scatter.7.cloned.1.call-done = bf16[128,512]{1,0:T(8,128)(2,1)} async-done(((bf16[4096,512]{1,0:T(8,128)(2,1)}), bf16[128,512]{1,0:T(8,128)(2,1)}) %reduce-scatter.7.cloned.1.call-update) | async-done | bytes 131088
  (216 shorter events, 72.4 us)
Async XLA Ops:
  7.2 46.0 %all-gather.8.cloned.1.call-start = ((), (), s32[]{:S(2)}) async-start(), calls=%async_computation.4 | async-start | bytes 1916928 | tf_op jit(solution)/shard_map/all_gather | solution.py:31
  7.9 128.9 %all-gather.4.cloned.1.call-start = ((), (), s32[]{:S(2)}) async-start(), calls=%async_computation.2 | async-start | bytes 1757184 | tf_op jit(solution)/shard_map/all_gather | solution.py:28
  8.6 206.2 %all-gather.6.cloned.1.call-start = ((), (), s32[]{:S(2)}) async-start(), calls=%async_computation.3 | async-start | bytes 1757184 | tf_op jit(solution)/shard_map/all_gather | solution.py:29
  9.4 447.5 %reduce-scatter.5.cloned.1.call-start = ((), (), s32[]{:S(2)}) async-start(), calls=%async_computation.5 | async-start | bytes 3514368 | tf_op jit(solution)/shard_map/reduce_scatter | solution.py:128
  335.2 1.5 copy-start
  335.3 252.6 %reduce-scatter.7.cloned.1.call-start = ((), (), s32[]{:S(2)}) async-start(), calls=%async_computation.6 | async-start | bytes 4325376
Sparse Core Ops, SparseCore 0:
  9.8 43.3 all-gather.7
  55.9 80.9 all-gather.3
  139.5 75.2 all-gather.5
  335.4 121.4 reduce-scatter.4
  461.5 126.2 reduce-scatter.6
where the time goes:
time: 596 us; the launch traced here: 594 us
  waiting for transfers between devices  438 us (73%)
  matrix products  108 us (18%)
  local copies, waits for them, and re-layouts  25.2 us (4%)
  between operations  13.9 us (2%)
  other arithmetic  7.38 us (1%)
    unnamed x6, waiting for transfers between devices  130 us
    reduce_scatter x1, waiting for transfers between devices, per_device(): lax.psum_scatter(kv_accum.astype(jnp.bfloat16), 'ctx', scatter_dimension=...  110 us
    all_gather x1, waiting for transfers between devices, per_device(): lax.all_gather(rotated_key_rows, 'ctx', axis=0, tiled=True)  79.3 us
    all_gather x1, waiting for transfers between devices, per_device(): lax.all_gather(value_matrix, 'ctx', axis=0, tiled=True)  78 us
    all_gather x1, waiting for transfers between devices, per_device(): grad_cols = lax.all_gather(out_grad, 'head', axis=1, tiled=True)  41 us
    dot_general x13, matrix products, forward_step(): jnp.einsum('tgrd,kgd->gtrk', q_tiles, key_tile, preferred_element_type=jn...  20.5 us
    dot_general x13, matrix products, grad_tile(): jnp.einsum('tgrd,kgd->gtrk', q_part, key_tile, preferred_element_type=jnp...  18.9 us
    dot_general x13, matrix products, grad_tile(): jnp.einsum('gtrk,kgd->tgrd', dscore, key_tile, preferred_element_type=jnp...  17.7 us
  transfers between devices with their start and end apart: 5, of which 5 were waited for; matrix products, arithmetic and copies ran while one was open for 3% of the time, Pallas kernels for 0%

commit v1 on v0

--- a/solution.py
+++ b/solution.py
@@ -25,7 +25,10 @@
     lo_seg = jnp.min(my_segs)
     q_tiles = queries.reshape(tok_rows, kv_heads, query_group_width, HEAD_SIZE)
     key_all, value_all = (
-        lax.all_gather(rotated_key_rows, "ctx", axis=0, tiled=True),
+        jnp.concatenate(
+            lax.all_to_all(jnp.stack([rotated_key_rows] * lax.axis_size("ctx")), "ctx", 0, 0),
+            axis=0,
+        ),
         lax.all_gather(value_matrix, "ctx", axis=0, tiled=True),
     )
     grad_cols = lax.all_gather(out_grad, "head", axis=1, tiled=True)

time: 596 us -> 494 us (0.83)
  waiting for transfers between devices: 438 us -> 360 us
  matrix products: 108 us -> 72.8 us
  starting transfers between devices: 0.19 us -> 11.6 us
    all_gather x1 -> x0, waiting for transfers between devices: 79.3 us -> none  [per_device(): lax.all_gather(rotated_key_rows, 'ctx', axis=0, tiled=True)]
    dot_general x13, matrix products: 18.9 us -> 7.12 us  [grad_tile(): jnp.einsum('tgrd,kgd->gtrk', q_part, key_tile, preferred_element_type=jnp...]
    dot_general x13, matrix products: 20.5 us -> 8.77 us  [forward_step(): jnp.einsum('tgrd,kgd->gtrk', q_tiles, key_tile, preferred_element_type=jn...]
    dot_general x13, matrix products: 17.7 us -> 5.97 us  [grad_tile(): jnp.einsum('gtrk,kgd->tgrd', dscore, key_tile, preferred_element_type=jnp...]
    all_to_all x0 -> x1, starting transfers between devices: none -> 11.4 us  [per_device(): lax.all_to_all(jnp.stack([rotated_key_rows] * lax.axis_size('ctx')), 'ctx...]
    all_gather x1, waiting for transfers between devices: 78 us -> 84.5 us  [per_device(): lax.all_gather(value_matrix, 'ctx', axis=0, tiled=True)]
    unnamed x6 -> x5, waiting for transfers between devices: 130 us -> 130 us
  transfers between devices with their start and end apart: 5 -> 5, of which waited for: 5 -> 4; matrix products, arithmetic and copies ran while one was open for 3% -> 4% of each run, Pallas kernels for 0% -> 0%
where the time goes in v1:
time: 494 us; the launch traced here: 493 us
  waiting for transfers between devices  360 us (73%)
  matrix products  72.8 us (15%)
  local copies, waits for them, and re-layouts  26 us (5%)
  between operations  13.9 us (3%)
  starting transfers between devices  11.6 us (2%)
  other arithmetic  6.73 us (1%)
    unnamed x5, waiting for transfers between devices  130 us
    reduce_scatter x1, waiting for transfers between devices, per_device(): lax.psum_scatter(kv_accum.astype(jnp.bfloat16), 'ctx', scatter_dimension=...  110 us
    all_gather x1, waiting for transfers between devices, per_device(): lax.all_gather(value_matrix, 'ctx', axis=0, tiled=True)  84.5 us
    all_gather x1, waiting for transfers between devices, per_device(): grad_cols = lax.all_gather(out_grad, 'head', axis=1, tiled=True)  36.4 us
    dot_general x13, matrix products, forward_step(): jnp.einsum('gtrk,kgd->tgrd', expo_vals.astype(jnp.bfloat16), value_tile,...  17.7 us
    dot_general x13, matrix products, grad_tile(): jnp.einsum('tgrd,kgd->gtrk', g_part, value_tile, preferred_element_type=j...  16.9 us
    all_to_all x1, starting transfers between devices, per_device(): lax.all_to_all(jnp.stack([rotated_key_rows] * lax.axis_size('ctx')), 'ctx...  11.4 us
    dynamic_update_slice x26, local copies, waits for them, and re-layouts, backward_step(): lax.dynamic_update_slice_in_dim(kv_accum, joined, offset, 0)  11.3 us
  transfers between devices with their start and end apart: 5, of which 4 were waited for; matrix products, arithmetic and copies ran while one was open for 4% of the time, Pallas kernels for 0%

profile of v1, /device:TPU:8, one launch (start us, length us, event | category | flops | bytes accessed | tf_op | source)
XLA Modules:
  0.0 492.7 jit_solution(12420677244109417904)
XLA Ops:
  8.6 2.2 stack.2
  10.9 11.4 %all-to-all-start = ((bf16[32,208,128]{2,1,0:T(8,128)(2,1)}), bf16[32,208,128]{2,1,0:T(8,128)(2,1)S(1)}, u32[]{:S(2)}, u32[]{:S(2)}) async-start(bf16[32,208,128]{2,1,0:T(8,128)(2,1)} %stack.2), calls=%async_computation | async-start | bytes 3407872 | tf_op jit(solution)/shard_map/all_to_all | solution.py:29
  22.9 36.4 %all-gather.5.cloned.1.call-done = bf16[208,4096]{1,0:T(8,128)(2,1)} async-done(((bf16[208,512]{1,0:T(8,128)(2,1)}), bf16[208,4096]{1,0:T(8,128)(2,1)}) %all-gather.5.cloned.1.call-update) | async-done | bytes 1703952 | tf_op jit(solution)/shard_map/all_gather | solution.py:34
  59.3 4.2 convolution_convert_fusion.1
  63.6 84.5 %all-gather.3.cloned.1.call-done = bf16[6656,128]{1,0:T(8,128)(2,1)} async-done(((bf16[208,128]{1,0:T(8,128)(2,1)}), bf16[6656,128]{1,0:T(8,128)(2,1)}) %all-gather.3.cloned.1.call-update) | async-done | bytes 1703952 | tf_op jit(solution)/shard_map/all_gather | solution.py:32
  148.1 29.4 %while.32 = (s32[]{:T(128)}, f32[208,1,4,128]{3,0,2,1:T(8,128)S(1)}, f32[1,208,4]{1,2,0:T(4,128)S(1)}, bf16[6656,128]{1,0:T(8,128)(2,1)}, s32[208]{0:T(256)S(1)}...) while((s32[]{:T(128)}, ...), condition=%wide.region_4.5_spmd.clone, body=%wide.region_2.4_spmd.clone.sunk | while | flops 220341792 | bytes 3264134 | solution.py:74
  149.0 1.4 fusion.58
  151.2 1.4 fusion.58
  153.5 1.4 fusion.58
  155.8 1.4 fusion.58
  158.0 1.4 fusion.58
  160.3 1.4 fusion.58
  162.6 1.4 fusion.58
  164.8 1.4 fusion.58
  167.1 1.4 fusion.58
  169.4 1.4 fusion.58
  171.6 1.4 fusion.58
  173.9 1.4 fusion.58
  176.2 1.4 fusion.58
  178.0 2.1 broadcast_in_dim.86.clone
  180.0 53.4 %while.33 = (s32[]{:T(128)}, f32[208,1,4,128]{3,0,2,1:T(8,128)S(1)}, bf16[6656,256]{1,0:T(8,128)(2,1)}, bf16[6656,128]{1,0:T(8,128)(2,1)S(1)}, s32[208]{0:T(256)...) while((s32[]{:T(128)}, ...), condition=%wide.region_7.8_spmd.clone, body=%wide.region_6.7_spmd.clone.sunk | while | flops 549298944 | bytes 11827109 | solution.py:128
  181.1 1.3 fusion.69
  183.4 0.8 constant_dynamic-update-slice_fusion.2
  185.2 1.3 fusion.69
  189.3 1.3 fusion.69
  191.6 0.7 constant_dynamic-update-slice_fusion.2
  193.4 1.3 fusion.69
  195.7 0.7 constant_dynamic-update-slice_fusion.2
  197.5 1.3 fusion.69
  201.6 1.3 fusion.69
  203.9 0.7 constant_dynamic-update-slice_fusion.2
  205.7 1.3 fusion.69
  209.8 1.3 fusion.69
  213.9 1.3 fusion.69
  216.2 0.8 constant_dynamic-update-slice_fusion.2
  218.1 1.3 fusion.69
  220.4 0.8 constant_dynamic-update-slice_fusion.2
  222.2 1.3 fusion.69
  224.5 0.7 constant_dynamic-update-slice_fusion.2
  226.3 1.3 fusion.69
  230.4 1.3 fusion.69
  233.6 1.3 copy-done
  234.9 3.3 fusion.29
  238.1 6.5 %copy.43 = bf16[4096,512]{1,0:T(8,128)(2,1)} copy(bf16[4096,512]{0,1:T(8,128)(2,1)} %fusion.29) | data formatting | bytes 8388608
  245.5 109.6 %reduce-scatter.5.cloned.1.call-done = bf16[208,256]{1,0:T(8,128)(2,1)} async-done(((bf16[6656,256]{1,0:T(8,128)(2,1)}), bf16[208,256]{1,0:T(8,128)(2,1)}) %reduce-scatter.5.cloned.1.call-update) | async-done | bytes 106512 | tf_op jit(solution)/shard_map/reduce_scatter | solution.py:131
  355.1 1.4 slice.14
  356.5 1.4 multiply_convert_fusion.1
  358.0 128.2 %reduce-scatter.7.cloned.1.call-done = bf16[128,512]{1,0:T(8,128)(2,1)} async-done(((bf16[4096,512]{1,0:T(8,128)(2,1)}), bf16[128,512]{1,0:T(8,128)(2,1)}) %reduce-scatter.7.cloned.1.call-update) | async-done | bytes 131088
  (220 shorter events, 44.9 us)
Async XLA Ops:
  7.2 52.1 %all-gather.5.cloned.1.call-start = ((), (), s32[]{:S(2)}) async-start(), calls=%async_computation.4 | async-start | bytes 1916928 | tf_op jit(solution)/shard_map/all_gather | solution.py:34
  7.9 140.2 %all-gather.3.cloned.1.call-start = ((), (), s32[]{:S(2)}) async-start(), calls=%async_computation.3 | async-start | bytes 1757184 | tf_op jit(solution)/shard_map/all_gather | solution.py:32
  10.9 11.5 %copy-start.2 = (s32[16]{0:T(128)S(1)}, s32[16]{0:T(128)}, u32[]{:S(2)}) copy-start(s32[16]{0:T(128)} %param.15) | copy-start | bytes 196
  10.9 11.8 %copy-start.1 = (bf16[208,512]{1,0:T(8,128)(2,1)S(1)}, bf16[208,512]{1,0:T(8,128)(2,1)}, u32[]{:S(2)}) copy-start(bf16[208,512]{1,0:T(8,128)(2,1)} %param.10) | copy-start | bytes 638980
  10.9 137.2 %all-to-all-start = ((bf16[32,208,128]{2,1,0:T(8,128)(2,1)}), bf16[32,208,128]{2,1,0:T(8,128)(2,1)S(1)}, u32[]{:S(2)}, u32[]{:S(2)}) async-start(bf16[32,208,128]{2,1,0:T(8,128)(2,1)} %stack.2), calls=%async_computation | async-start | bytes 3407872 | tf_op jit(solution)/shard_map/all_to_all | solution.py:29
  22.3 332.7 %reduce-scatter.5.cloned.1.call-start = ((), (), s32[]{:S(2)}) async-start(), calls=%async_computation.5 | async-start | bytes 3514368 | tf_op jit(solution)/shard_map/reduce_scatter | solution.py:131
  233.4 1.5 copy-start
  233.4 252.7 %reduce-scatter.7.cloned.1.call-start = ((), (), s32[]{:S(2)}) async-start(), calls=%async_computation.6 | async-start | bytes 4325376
Sparse Core Ops, SparseCore 0:
  9.8 49.4 all-gather.4
  61.9 86.1 all-gather.2
  233.6 121.4 reduce-scatter.4
  359.7 126.3 reduce-scatter.6
